TPU v7x, 32 devices: a whole 2x2x4 slice. The times are simulated.
32 devices in a mesh: dp: 8 (over z, x), tensor: 4 (over y, core).
Axes of the slice: x: 2, y: 2, z: 4, core: 2. Of those that a mesh axis runs over, the one named last changes fastest.
Arguments:
- residual: float32 [4096, 1024], P(('dp', 'tensor')), may hold values from -6 to 6
- segments: int32 [8, 512], P('dp'), may hold values from 0 to 10, never falling along the last dimension, each value on 1 to 256 neighbouring positions
- norm_gain: float32 [1024], replicated, may hold values from 0.5 to 1.5
- in_gate: bfloat16 [1024, 2048], P('dp', 'tensor'), may hold values from -0.1875 to 0.1875
- in_value: bfloat16 [1024, 2048], P('dp', 'tensor'), may hold values from -0.1875 to 0.1875
- in_step: bfloat16 [1024, 32], P('dp', 'tensor'), may hold values from -0.1875 to 0.1875
- in_state: bfloat16 [1024, 256], P('dp'), may hold values from -0.1875 to 0.1875
- kernel_value: float32 [4, 2048], P(None, 'tensor'), may hold values from -3 to 3
- bias_value: float32 [2048], P('tensor'), may hold values from -1.5 to 1.5
- kernel_state: float32 [4, 256], replicated, may hold values from -3 to 3
- bias_state: float32 [256], replicated, may hold values from -1.5 to 1.5
- step_bias: float32 [32], P('tensor'), may hold values from -5 to -1
- log_decay: float32 [32], P('tensor'), may hold values from -1 to 2.5
- skip_gain: float32 [32], P('tensor'), may hold values from 0.5 to 1.5
- gate_gain: float32 [2048], P('tensor'), may hold values from 0.5 to 1.5
- out_proj: bfloat16 [1024, 2048], P('dp', 'tensor'), may hold values from -0.125 to 0.125
- cotangent: float32 [4096, 1024], P(('dp', 'tensor')), may hold values from -6 to 6
Outputs:
- layer_out: float32 [4096, 1024], P(('dp', 'tensor'))
- grad_input: float32 [4096, 1024], P(('dp', 'tensor'))
- grad_norm_gain: float32 [1024], replicated
- grad_in_gate: float32 [1024, 2048], P('dp', 'tensor')
- grad_in_value: float32 [1024, 2048], P('dp', 'tensor')
- grad_in_step: float32 [1024, 32], P('dp', 'tensor')
- grad_in_state: float32 [1024, 256], P('dp', 'tensor')
- grad_kernel_value: float32 [4, 2048], P(None, 'tensor')
- grad_bias_value: float32 [2048], P('tensor')
- grad_kernel_state: float32 [4, 256], replicated
- grad_bias_state: float32 [256], replicated
- grad_step_bias: float32 [32], P('tensor')
- grad_log_decay: float32 [32], P('tensor')
- grad_skip_gain: float32 [32], P('tensor')
- grad_gate_gain: float32 [2048], P('tensor')
- grad_out_proj: float32 [1024, 2048], P('dp', 'tensor')
Inputs may be any that keep to these rules, and one draw needn't show every extreme that they name: `segments`: segment numbers start at 0 in each packed row and never fall along it; one segment of each row holds exactly 256 tokens, none more.
All inputs are finite; a program needn't handle non-finite values.
Results may differ from a plain program's by a relative error of at most 0.0083.
Values may be sent and summed in bfloat16 or wider, within the bound.
A program may use at most 128 MiB of HBM per device.

v0:
```python
from functools import partial

import jax
import jax.numpy as jnp
from jax import lax
from jax.experimental import pallas as pl
from jax.experimental.pallas import tpu as pltpu
from jax.sharding import PartitionSpec as P

epsilon = 1e-05
precise = lax.Precision.HIGHEST
MESH = pl.DeviceIdType.MESH
VM = pl.BlockSpec(memory_space=pltpu.VMEM)
F32 = jnp.float32
BF16 = jnp.bfloat16


def loop(begin, end, step):
    def body(k, carry):
        step(k)
        return carry

    lax.fori_loop(begin, end, body, 0)


def halves(cols):
    left = (cols // 128 + 1) // 2 * 128
    return pl.ds(0, left), pl.ds(left, cols - left)


def dev(d, t):
    return (d, t)


def push(src, dst, ssem, rsem, d, t):
    return pltpu.make_async_remote_copy(
        src_ref=src,
        dst_ref=dst,
        send_sem=ssem,
        recv_sem=rsem,
        device_id=dev(d, t),
        device_id_type=MESH,
    )


def greet_tensor(t_size, barrier):
    d = lax.axis_index("dp")
    t = lax.axis_index("tensor")
    for k in range(1, t_size):
        pl.semaphore_signal(
            barrier, inc=1, device_id=dev(d, lax.rem(t + k, t_size)), device_id_type=MESH
        )


def greet_dp(n, barrier):
    d = lax.axis_index("dp")
    t = lax.axis_index("tensor")

    def signal(k):
        pl.semaphore_signal(
            barrier, inc=1, device_id=dev(lax.rem(d + k, n), t), device_id_type=MESH
        )

    loop(1, n, signal)


def gather_kernel(
    n, t_size, a_ref, c_ref, w_ref, ga, gc, gw, sa, ra, sc, rc, sx, su, sd, rw
):
    d = lax.axis_index("dp")
    t = lax.axis_index("tensor")
    hi = d // 2
    lo = lax.rem(d, 2)
    line = n // 2
    parts = halves(w_ref.shape[1])
    everything = pl.ds(0, w_ref.shape[0])
    barrier = pltpu.get_barrier_semaphore()
    greet_tensor(t_size, barrier)
    greet_dp(n, barrier)
    pl.semaphore_wait(barrier, n + t_size - 2)
    mate = d + 1 - 2 * lo

    def at(h):
        return everything, parts[h]

    def own(h, sems, to):
        return push(w_ref.at[at(h)], gw.at[(d,) + at(h)], sems.at[h, d], rw.at[h, d], to, t)

    def relay(h, q, sems, to):
        return push(
            gw.at[(q,) + at(h)], gw.at[(q,) + at(h)], sems.at[h, q], rw.at[h, q], to, t
        )

    def arrive(h, q):
        push(
            gw.at[(q,) + at(h)], gw.at[(q,) + at(h)], sx.at[h, q], rw.at[h, q], mate, t
        ).wait_recv()

    has_up = hi < line - 1
    has_down = hi > 0
    own(0, sx, mate).start()
    for k in range(1, t_size):
        other = lax.rem(t + k, t_size)
        push(a_ref, ga.at[t], sa.at[other], ra.at[t], d, other).start()

    @pl.when(has_up)
    def _():
        own(1, su, d + 2).start()
        own(0, su, d + 2).start()

    @pl.when(has_down)
    def _():
        own(1, sd, d - 2).start()
        own(0, sd, d - 2).start()

    own(1, sx, mate).start()
    for k in range(1, t_size):
        other = lax.rem(t + k, t_size)
        push(c_ref, gc.at[t], sc.at[other], rc.at[t], d, other).start()
    gw[d] = w_ref[...]
    ga[t] = a_ref[...]
    gc[t] = c_ref[...]
    arrive(0, mate)

    @pl.when(has_up)
    def _():
        relay(0, mate, su, d + 2).start()

    @pl.when(has_down)
    def _():
        relay(0, mate, sd, d - 2).start()

    def step(k):
        for below in (True, False):
            far = d - 2 * k if below else d + 2 * k
            far_mate = mate - 2 * k if below else mate + 2 * k
            exists = hi >= k if below else hi + k < line
            onward = jnp.logical_and(exists, has_up if below else has_down)
            sems = su if below else sd
            to = d + 2 if below else d - 2

            @pl.when(exists)
            def _():
                arrive(1, far)
                relay(1, far, sx, mate).start()

            @pl.when(onward)
            def _():
                relay(1, far, sems, to).start()

            for q in (far, far_mate):

                @pl.when(exists)
                def _():
                    arrive(0, q)

                @pl.when(onward)
                def _():
                    relay(0, q, sems, to).start()

    loop(1, line, step)
    own(0, sx, mate).wait_send()

    def finish(k):
        arrive(1, 2 * k + 1 - lo)
        relay(1, 2 * k + lo, sx, mate).wait_send()

        @pl.when(jnp.logical_and(has_up, hi >= k))
        def _():
            relay(1, 2 * k + lo, su, mate).wait_send()
            for j in range(2):
                relay(0, 2 * k + j, su, mate).wait_send()

        @pl.when(jnp.logical_and(has_down, hi <= k))
        def _():
            relay(1, 2 * k + lo, sd, mate).wait_send()
            for j in range(2):
                relay(0, 2 * k + j, sd, mate).wait_send()

    loop(0, line, finish)
    for k in range(1, t_size):
        other = lax.rem(t + k, t_size)
        push(a_ref, ga.at[other], sa.at[other], ra.at[other], d, other).wait()
        push(c_ref, gc.at[other], sc.at[other], rc.at[other], d, other).wait()


def gather_all(n, t_size, a, c, w):
    dma = pltpu.SemaphoreType.DMA
    return pl.pallas_call(
        partial(gather_kernel, n, t_size),
        out_shape=(
            jax.ShapeDtypeStruct((t_size,) + a.shape, a.dtype),
            jax.ShapeDtypeStruct((t_size,) + c.shape, c.dtype),
            jax.ShapeDtypeStruct((n,) + w.shape, w.dtype),
        ),
        in_specs=[VM] * 3,
        out_specs=(VM, VM, VM),
        scratch_shapes=[dma((t_size,))] * 4 + [dma((2, n))] * 4,
        compiler_params=pltpu.CompilerParams(collective_id=0, has_side_effects=True),
    )(a, c, w)


def spread_kernel(t_size, scatter, x_ref, out_ref, ss, rs):
    d = lax.axis_index("dp")
    t = lax.axis_index("tensor")
    barrier = pltpu.get_barrier_semaphore()
    greet_tensor(t_size, barrier)
    pl.semaphore_wait(barrier, t_size - 1)
    for k in range(1, t_size):
        other = lax.rem(t + k, t_size)
        src = x_ref.at[other] if scatter else x_ref
        push(src, out_ref.at[t], ss.at[other], rs.at[t], d, other).start()
    out_ref[t] = x_ref[t] if scatter else x_ref[...]
    for k in range(1, t_size):
        other = lax.rem(t + k, t_size)
        src = x_ref.at[other] if scatter else x_ref
        push(src, out_ref.at[other], ss.at[other], rs.at[other], d, other).wait()


def spread_tensor(t_size, x, scatter, cid):
    dma = pltpu.SemaphoreType.DMA
    shape = x.shape if scatter else (t_size,) + x.shape
    return pl.pallas_call(
        partial(spread_kernel, t_size, scatter),
        out_shape=jax.ShapeDtypeStruct(shape, x.dtype),
        in_specs=[VM],
        out_specs=VM,
        scratch_shapes=[dma((t_size,))] * 2,
        compiler_params=pltpu.CompilerParams(collective_id=cid, has_side_effects=True),
    )(x)


def reduce_kernel(
    n,
    t_size,
    w_ref,
    l_ref,
    g_ref,
    res_ref,
    gain_ref,
    cot_ref,
    sd_ref,
    st_ref,
    w_out,
    l_out,
    gi_out,
    sd_out,
    st_out,
    rl,
    rg,
    rx0,
    rx1,
    ru1,
    rd1,
    ru0,
    rd0,
    bu1,
    bd1,
    bu0,
    bd0,
    bx1,
    st_mine,
    rst,
    st_sum,
    rst_dp,
    rsd,
    s_l,
    q_l,
    s_g,
    q_g,
    s_x0,
    q_x0,
    s_x1,
    q_x1,
    s_u1,
    q_u1,
    s_d1,
    q_d1,
    s_u0,
    q_u0,
    s_d0,
    q_d0,
    s_st,
    q_st,
    s_sp,
    q_sp,
    s_sd,
    q_sd,
):
    d = lax.axis_index("dp")
    t = lax.axis_index("tensor")
    hi = d // 2
    lo = lax.rem(d, 2)
    line = n // 2
    mate = d + 1 - 2 * lo
    rows = w_ref.shape[1]
    every = pl.ds(0, rows)
    top, low = halves(w_ref.shape[2])
    barrier = pltpu.get_barrier_semaphore()
    greet_tensor(t_size, barrier)
    greet_dp(n, barrier)
    pl.semaphore_wait(barrier, n + t_size - 2)
    has_up = hi < line - 1
    has_down = hi > 0

    def send_x0(k):
        return push(
            w_ref.at[2 * k + 1 - lo, every, top], rx0.at[k], s_x0.at[k], q_x0.at[k], mate, t
        )

    loop(0, line, lambda k: send_x0(k).start())

    def tensor_send(src, buf, ss, qs, other):
        return push(src.at[other], buf.at[t], ss.at[other], qs.at[t], d, other)

    for k in range(1, t_size):
        other = lax.rem(t + k, t_size)
        tensor_send(g_ref, rg, s_g, q_g, other).start()

    def sd_send(q):
        return push(sd_ref, rsd.at[d], s_sd.at[q], q_sd.at[d], q, t)

    loop(1, n, lambda k: sd_send(lax.rem(d + k, n)).start())
    for k in range(1, t_size):
        other = lax.rem(t + k, t_size)
        tensor_send(l_ref, rl, s_l, q_l, other).start()

    def hop(buf, got, ss, qs, k, to):
        return push(buf.at[k], got.at[k], ss.at[k], qs.at[k], to, t)

    def chain(k, mine, up):
        has_prev = has_down if up else has_up
        buf, got, ss, qs, to = (
            (mine[1], mine[2], mine[3], mine[4], d + 2)
            if up
            else (mine[5], mine[6], mine[7], mine[8], d - 2)
        )

        @pl.when(k > hi if up else k < hi)
        def _():
            @pl.when(has_prev)
            def _():
                hop(buf, got, ss, qs, k, to).wait_recv()
                buf[k] = (mine[0](k) + got[k].astype(F32)).astype(BF16)

            @pl.when(jnp.logical_not(has_prev))
            def _():
                buf[k] = mine[0](k).astype(BF16)

            hop(buf, got, ss, qs, k, to).start()

    def pair(k):
        return w_ref[pl.ds(2 * k, 2), :, low].astype(F32)

    set1 = (pair, bu1, ru1, s_u1, q_u1, bd1, rd1, s_d1, q_d1)

    def joined(k):
        return w_ref[2 * k + lo, :, top].astype(F32) + rx0[k].astype(F32)

    set0 = (joined, bu0, ru0, s_u0, q_u0, bd0, rd0, s_d0, q_d0)

    def walk1(k):
        chain(line - 1 - k, set1, True)
        chain(k, set1, False)

    loop(0, line - 1, walk1)

    g_sum = g_ref[t].astype(F32)
    for k in range(1, t_size):
        other = lax.rem(t + k, t_size)
        push(g_ref.at[other], rg.at[other], s_g.at[other], q_g.at[other], d, other).wait()
        g_sum = g_sum + rg[other].astype(F32)
    res = res_ref[...]
    inv = lax.rsqrt(jnp.mean(res * res, axis=1, keepdims=True) + epsilon)
    unit = res * inv
    scaled = g_sum * gain_ref[...]
    inner = jnp.mean(scaled * unit, axis=1, keepdims=True)
    gi_out[...] = cot_ref[...] + inv * (scaled - unit * inner)
    st_mine[...] = st_ref[...]
    st_mine[0:1] = jnp.sum(g_sum * unit, axis=0, keepdims=True)

    def st_send(other):
        return push(st_mine, rst.at[t], s_st.at[other], q_st.at[t], d, other)

    for k in range(1, t_size):
        st_send(lax.rem(t + k, t_size)).start()

    loop(
        0,
        line,
        lambda k: push(rx0.at[k], rx0.at[k], s_x0.at[k], q_x0.at[k], mate, t).wait_recv(),
    )

    def walk0(k):
        chain(line - 1 - k, set0, True)
        chain(k, set0, False)

    loop(0, line - 1, walk0)

    w_out[:, low] = w_ref[d, :, low].astype(F32)
    bx1[...] = w_ref[mate, :, low]

    @pl.when(has_down)
    def _():
        hop(bu1, ru1, s_u1, q_u1, hi, d).wait_recv()
        w_out[:, low] = w_out[:, low] + ru1[hi, lo].astype(F32)
        bx1[...] = (bx1[...].astype(F32) + ru1[hi, 1 - lo].astype(F32)).astype(BF16)

    @pl.when(has_up)
    def _():
        hop(bd1, rd1, s_d1, q_d1, hi, d).wait_recv()
        w_out[:, low] = w_out[:, low] + rd1[hi, lo].astype(F32)
        bx1[...] = (bx1[...].astype(F32) + rd1[hi, 1 - lo].astype(F32)).astype(BF16)

    send_x1 = push(bx1, rx1, s_x1.at[0], q_x1.at[0], mate, t)
    send_x1.start()

    st_total = st_mine[...]
    for k in range(1, t_size):
        other = lax.rem(t + k, t_size)
        push(st_mine, rst.at[other], s_st.at[other], q_st.at[other], d, other).wait()
        st_total = st_total + rst[other]
    st_sum[...] = st_total

    def sp_send(q):
        return push(st_sum, rst_dp.at[d], s_sp.at[q], q_sp.at[d], q, t)

    loop(1, n, lambda k: sp_send(lax.rem(d + k, n)).start())

    l_sum = l_ref[t].astype(F32)
    for k in range(1, t_size):
        other = lax.rem(t + k, t_size)
        push(l_ref.at[other], rl.at[other], s_l.at[other], q_l.at[other], d, other).wait()
        l_sum = l_sum + rl[other].astype(F32)
    l_out[...] = res_ref[...] + l_sum

    w_out[:, top] = joined(hi)

    @pl.when(has_down)
    def _():
        hop(bu0, ru0, s_u0, q_u0, hi, d).wait_recv()
        w_out[:, top] = w_out[:, top] + ru0[hi].astype(F32)

    @pl.when(has_up)
    def _():
        hop(bd0, rd0, s_d0, q_d0, hi, d).wait_recv()
        w_out[:, top] = w_out[:, top] + rd0[hi].astype(F32)

    send_x1.wait()
    w_out[:, low] = w_out[:, low] + rx1[...].astype(F32)

    rsd[d] = sd_ref[...]
    rst_dp[d] = st_sum[...]

    def settle(k):
        q = lax.rem(d + k, n)
        push(sd_ref, rsd.at[q], s_sd.at[q], q_sd.at[q], q, t).wait()
        push(st_sum, rst_dp.at[q], s_sp.at[q], q_sp.at[q], q, t).wait()

    loop(1, n, settle)
    sd_out[...] = jnp.sum(rsd[...], axis=0)
    st_out[...] = jnp.sum(rst_dp[...], axis=0)

    def drain(k):
        send_x0(k).wait_send()

        @pl.when(k > hi)
        def _():
            hop(bu1, ru1, s_u1, q_u1, k, d).wait_send()
            hop(bu0, ru0, s_u0, q_u0, k, d).wait_send()

        @pl.when(k < hi)
        def _():
            hop(bd1, rd1, s_d1, q_d1, k, d).wait_send()
            hop(bd0, rd0, s_d0, q_d0, k, d).wait_send()

    loop(0, line, drain)


def reduce_all(n, t_size, w, l, g, res, gain, cot, small_d, small_t):
    dma = pltpu.SemaphoreType.DMA
    vm = pltpu.VMEM
    rows, cols = w.shape[1:]
    line = n // 2
    left = halves(cols)[0].size
    two = vm((line, 2, rows, cols - left), BF16)
    one = vm((line, rows, left), BF16)
    tok = vm(l.shape, BF16)
    struct = jax.ShapeDtypeStruct
    t_sem = dma((t_size,))
    k_sem = dma((line,))
    n_sem = dma((n,))
    return pl.pallas_call(
        partial(reduce_kernel, n, t_size),
        out_shape=(
            struct((rows, cols), F32),
            struct(res.shape, F32),
            struct(res.shape, F32),
            struct(small_d.shape, F32),
            struct(small_t.shape, F32),
        ),
        in_specs=[VM] * 8,
        out_specs=(VM,) * 5,
        scratch_shapes=[
            tok,
            tok,
            one,
            vm((rows, cols - left), BF16),
            two,
            two,
            one,
            one,
            two,
            two,
            one,
            one,
            vm((rows, cols - left), BF16),
            vm(small_t.shape, F32),
            vm((t_size,) + small_t.shape, F32),
            vm(small_t.shape, F32),
            vm((n,) + small_t.shape, F32),
            vm((n,) + small_d.shape, F32),
        ]
        + [t_sem] * 4
        + [k_sem] * 2
        + [dma((1,))] * 2
        + [k_sem] * 8
        + [t_sem] * 2
        + [n_sem] * 4,
        compiler_params=pltpu.CompilerParams(collective_id=3, has_side_effects=True),
    )(w, l, g, res, gain, cot, small_d, small_t)


def dot_f(a, b, dims, precision=None):
    return lax.dot_general(
        a, b, ((dims[0], dims[1]), ((), ())), preferred_element_type=F32, precision=precision
    )


def decay_of(cum_col, cum_row, allowed):
    return jnp.where(allowed, jnp.exp(jnp.where(allowed, cum_col - cum_row, 0.0)), 0.0)


def allowed_of(seg_col, seg_row):
    size = seg_col.shape[0]
    row_pos = lax.broadcasted_iota(jnp.int32, (size, size), 0)
    col_pos = lax.broadcasted_iota(jnp.int32, (size, size), 1)
    return (seg_col == seg_row) & (col_pos <= row_pos)


def pick(ref, head):
    lanes = lax.broadcasted_iota(jnp.int32, ref.shape, 1)
    return jnp.sum(jnp.where(lanes == head, ref[...], 0.0), axis=1, keepdims=True)


def mix_kernel(
    width, x_ref, b_ref, c_ref, cum_ref, cumt_ref, step_ref, skip_ref, sc_ref, sr_ref, y_ref, scores
):
    j = pl.program_id(0)
    allowed = allowed_of(sc_ref[...], sr_ref[...])

    @pl.when(j == 0)
    def _():
        scores[...] = dot_f(c_ref[...], b_ref[...], ((1,), (1,)), precise)

    count = x_ref.shape[1] // width
    for i in range(count):
        head = j * count + i
        x = x_ref[:, i * width : (i + 1) * width]
        decay = decay_of(pick(cum_ref, head), cumt_ref[pl.ds(head, 1), :], allowed)
        mixing = (scores[...] * decay).astype(BF16)
        fed = (x * pick(step_ref, head)).astype(BF16)
        y = dot_f(mixing, fed, ((1,), (0,)))
        y_ref[:, i * width : (i + 1) * width] = y + pick(skip_ref, head) * x


def mix_forward(x, b, c, cum, step, skip, seg, width):
    tokens, channels = x.shape
    pairs = channels // 128
    whole = lambda a: pl.BlockSpec(a.shape, lambda j: (0,) * a.ndim)
    block = pl.BlockSpec((tokens, 128), lambda j: (0, j))
    args = (x, b, c, cum, cum.T, step, skip[None, :], seg[:, None], seg[None, :])
    return pl.pallas_call(
        partial(mix_kernel, width),
        grid=(pairs,),
        out_shape=jax.ShapeDtypeStruct(x.shape, F32),
        in_specs=[block] + [whole(a) for a in args[1:]],
        out_specs=block,
        scratch_shapes=[pltpu.VMEM((tokens, tokens), F32)],
    )(*args)


def back_kernel(
    width,
    x_ref,
    dy_ref,
    b_ref,
    c_ref,
    cum_ref,
    cumt_ref,
    step_ref,
    skip_ref,
    sc_ref,
    sr_ref,
    dx_ref,
    db_ref,
    dc_ref,
    row_ref,
    col_ref,
    dstep_ref,
    dskip_ref,
    scores,
    d_scores,
):
    j = pl.program_id(0)
    allowed = allowed_of(sc_ref[...], sr_ref[...])

    @pl.when(j == 0)
    def _():
        scores[...] = dot_f(c_ref[...], b_ref[...], ((1,), (1,)), precise)
        d_scores[...] = jnp.zeros_like(d_scores)
        row_ref[...] = jnp.zeros_like(row_ref)
        dstep_ref[...] = jnp.zeros_like(dstep_ref)
        dskip_ref[...] = jnp.zeros_like(dskip_ref)

    lanes = lax.broadcasted_iota(jnp.int32, row_ref.shape, 1)
    count = x_ref.shape[1] // width
    for i in range(count):
        head = j * count + i
        x = x_ref[:, i * width : (i + 1) * width]
        dy = dy_ref[:, i * width : (i + 1) * width]
        step = pick(step_ref, head)
        decay = decay_of(pick(cum_ref, head), cumt_ref[pl.ds(head, 1), :], allowed)
        mixing = scores[...] * decay
        fed = (x * step).astype(BF16)
        dy_half = dy.astype(BF16)
        d_mix = dot_f(dy_half, fed, ((1,), (1,)))
        d_fed = dot_f(mixing.astype(BF16), dy_half, ((0,), (0,)))
        d_scores[...] += d_mix * decay
        energy = d_mix * mixing
        hot = lanes == head
        row_ref[...] += jnp.where(hot, jnp.sum(energy, axis=1, keepdims=True), 0.0)
        col_ref[pl.ds(head, 1), :] = jnp.sum(energy, axis=0, keepdims=True)
        dstep_ref[...] += jnp.where(hot, jnp.sum(d_fed * x, axis=1, keepdims=True), 0.0)
        dskip_ref[...] += jnp.where(hot, jnp.sum(dy * x, axis=1, keepdims=True), 0.0)
        dx_ref[:, i * width : (i + 1) * width] = d_fed * step + pick(skip_ref, head) * dy

    @pl.when(j == pl.num_programs(0) - 1)
    def _():
        grad = d_scores[...].astype(BF16)
        dc_ref[...] = dot_f(grad, b_ref[...].astype(BF16), ((1,), (0,)))
        db_ref[...] = dot_f(grad, c_ref[...].astype(BF16), ((0,), (0,)))


def mix_backward(x, dy, b, c, cum, step, skip, seg, width):
    tokens, channels = x.shape
    heads = cum.shape[1]
    pairs = channels // 128
    whole = lambda a: pl.BlockSpec(a.shape, lambda j: (0,) * a.ndim)
    block = pl.BlockSpec((tokens, 128), lambda j: (0, j))
    struct = jax.ShapeDtypeStruct
    args = (x, dy, b, c, cum, cum.T, step, skip[None, :], seg[:, None], seg[None, :])
    outs = (
        struct(x.shape, F32),
        struct(b.shape, F32),
        struct(c.shape, F32),
        struct((tokens, heads), F32),
        struct((heads, tokens), F32),
        struct((tokens, heads), F32),
        struct((tokens, heads), F32),
    )
    return pl.pallas_call(
        partial(back_kernel, width),
        grid=(pairs,),
        out_shape=outs,
        in_specs=[block, block] + [whole(a) for a in args[2:]],
        out_specs=(block,) + tuple(whole(a) for a in outs[1:]),
        scratch_shapes=[pltpu.VMEM((tokens, tokens), F32)] * 2,
    )(*args)


def conv_silu(values, kernel, shift_bias, seg_ids):
    taps = kernel.shape[0]
    length = values.shape[0]
    padded = jnp.pad(values, ((taps - 1, 0), (0, 0)))
    seg_pad = jnp.concatenate([jnp.full((taps - 1,), -1, jnp.int32), seg_ids])
    summed = jnp.zeros_like(values) + shift_bias
    for offset in range(taps):
        begin_at = taps - 1 - offset
        shifted = padded[begin_at : begin_at + length]
        same_doc = (seg_pad[begin_at : begin_at + length] == seg_ids).astype(values.dtype)
        summed = summed + kernel[offset] * shifted * same_doc[:, None]
    return jax.nn.silu(summed)


def local(
    n,
    t_size,
    residual,
    segments,
    norm_gain,
    in_gate,
    in_value,
    in_step,
    in_state,
    kernel_value,
    bias_value,
    kernel_state,
    bias_state,
    step_bias,
    log_decay,
    skip_gain,
    gate_gain,
    out_proj,
    cotangent,
):
    seg_ids = segments[0]
    width = in_gate.shape[1]
    heads = in_step.shape[1]
    states = in_state.shape[1]
    model = residual.shape[1]
    inner = width * t_size
    rows = in_gate.shape[0]
    tokens = seg_ids.shape[0]
    t = lax.axis_index("tensor")

    inv = lax.rsqrt(jnp.mean(residual * residual, axis=1, keepdims=True) + epsilon)
    normed = (residual * inv * norm_gain).astype(BF16)
    cot_half = cotangent.astype(BF16)
    step_pad = -heads % 128
    w_mine = jnp.concatenate(
        [
            in_gate,
            in_value,
            in_state,
            in_step,
            jnp.zeros((rows, step_pad), BF16),
            out_proj,
        ],
        axis=1,
    )
    full_rows, cot_full, w_full = gather_all(n, t_size, normed, cot_half, w_mine)
    full_rows = full_rows.reshape(tokens, model)
    cot_full = cot_full.reshape(tokens, model)
    w_full = w_full.reshape(model, w_mine.shape[1])
    s1, s2 = 2 * width, 2 * width + states
    s3 = s2 + heads
    out_full = w_full[:, s3 + step_pad :]

    projected = jnp.dot(full_rows, w_full[:, : s3 + step_pad], preferred_element_type=F32)
    gate_raw = projected[:, :width]
    value_raw = projected[:, width:s1]
    state_raw = projected[:, s1:s2]
    step_raw = projected[:, s2:s3]
    conv_value, value_pull = jax.vjp(
        partial(conv_silu, seg_ids=seg_ids), value_raw, kernel_value, bias_value
    )
    conv_state = conv_silu(state_raw, kernel_state, bias_state, seg_ids)
    part = states // 2
    write_vec, read_vec = conv_state[:, :part], conv_state[:, part:]
    step_in = step_raw + step_bias
    step_size = jax.nn.softplus(step_in)
    rate = -jnp.exp(log_decay)
    log_keep = rate * step_size
    tri = jnp.tril(jnp.ones((tokens, tokens), F32))
    cum = jnp.dot(tri, log_keep, precision=precise)
    head_width = width // heads
    mixer_out = mix_forward(
        conv_value, write_vec, read_vec, cum, step_size, skip_gain, seg_ids, head_width
    )

    sig_gate = jax.nn.sigmoid(gate_raw)
    gate_act = gate_raw * sig_gate
    gated = mixer_out * gate_act
    grad_gate_normed = jnp.dot(cot_full, out_full, preferred_element_type=F32)
    scaled = grad_gate_normed * gate_gain
    sums = jnp.concatenate(
        [
            jnp.sum(gated * gated, axis=1).reshape(-1, 128),
            jnp.sum(scaled * gated, axis=1).reshape(-1, 128),
        ],
        axis=0,
    )
    totals = jnp.sum(spread_tensor(t_size, sums, False, 1), axis=0)
    split = tokens // 128
    total_sq = totals[:split].reshape(tokens)
    total_dot = totals[split:].reshape(tokens)
    inv_rms = lax.rsqrt(total_sq / inner + epsilon)[:, None]
    gate_normed = (gated * inv_rms * gate_gain).astype(BF16)
    grad_gate_gain = jnp.sum(grad_gate_normed * gated * inv_rms, axis=0)
    grad_gated = inv_rms * scaled - gated * inv_rms**3 * (total_dot / inner)[:, None]
    grad_mixer_out = grad_gated * gate_act
    grad_gate_raw = grad_gated * mixer_out * sig_gate * (1.0 + gate_raw * (1.0 - sig_gate))

    grad_conv_value, grad_b, grad_c, row_e, col_e, d_fed_step, d_skip = mix_backward(
        conv_value,
        grad_mixer_out,
        write_vec,
        read_vec,
        cum,
        step_size,
        skip_gain,
        seg_ids,
        head_width,
    )
    slice_width = states // t_size
    grad_bc = jnp.concatenate([grad_b, grad_c], axis=1).astype(BF16)
    pieces = grad_bc.reshape(tokens, t_size, slice_width).transpose(1, 0, 2)
    grad_conv_state = jnp.sum(
        spread_tensor(t_size, pieces, True, 2).astype(F32), axis=0
    )
    d_keep = lax.dot_general(
        tri, row_e - col_e.T, (((0,), (0,)), ((), ())), precision=precise
    )
    grad_step_raw = (d_fed_step + d_keep * rate) * jax.nn.sigmoid(step_in)
    grad_step_bias = jnp.sum(grad_step_raw, axis=0)
    grad_log_decay = jnp.sum(d_keep * log_keep, axis=0)
    grad_skip = jnp.sum(d_skip, axis=0)

    grad_value_raw, grad_kernel_value, grad_bias_value = value_pull(grad_conv_value)
    begin = t * slice_width
    unused, state_pull = jax.vjp(
        partial(conv_silu, seg_ids=seg_ids),
        lax.dynamic_slice_in_dim(state_raw, begin, slice_width, 1),
        lax.dynamic_slice_in_dim(kernel_state, begin, slice_width, 1),
        lax.dynamic_slice_in_dim(bias_state, begin, slice_width, 0),
    )
    grad_state_slice, grad_ks, grad_bs = state_pull(grad_conv_state)
    state_cols = lax.dynamic_slice_in_dim(w_full[:, s1:s2], begin, slice_width, 1)

    fill = -(slice_width + heads) % 128
    grad_projected = jnp.concatenate(
        [
            grad_gate_raw,
            grad_value_raw,
            grad_state_slice,
            grad_step_raw,
            jnp.zeros((tokens, fill), F32),
        ],
        axis=1,
    ).astype(BF16)
    back_cat = jnp.concatenate(
        [w_full[:, :s1], state_cols, w_full[:, s2:s3], jnp.zeros((model, fill), BF16)], axis=1
    )
    grad_normed = lax.dot_general(
        grad_projected, back_cat, (((1,), (1,)), ((), ())), preferred_element_type=F32
    ).astype(BF16)
    layer_part = lax.dot_general(
        gate_normed, out_full, (((1,), (1,)), ((), ())), preferred_element_type=F32
    ).astype(BF16)
    grad_weights = lax.dot_general(
        full_rows, grad_projected, (((0,), (0,)), ((), ())), preferred_element_type=F32
    ).astype(BF16)
    grad_out = lax.dot_general(
        cot_full, gate_normed, (((0,), (0,)), ((), ())), preferred_element_type=F32
    ).astype(BF16)
    grads = jnp.concatenate([grad_weights, grad_out], axis=1).reshape(n, rows, -1)

    misc = jnp.concatenate([grad_step_bias, grad_log_decay, grad_skip])
    misc = jnp.pad(misc, (0, width - misc.shape[0]))
    small_d = jnp.concatenate(
        [grad_kernel_value, grad_bias_value[None], grad_gate_gain[None], misc[None]], axis=0
    )
    small_d = jnp.pad(small_d, ((0, -small_d.shape[0] % 8), (0, 0)))
    taps = kernel_state.shape[0]
    state_grads = lax.dynamic_update_slice_in_dim(
        jnp.zeros((taps + 1, states), F32),
        jnp.concatenate([grad_ks, grad_bs[None]], axis=0),
        begin,
        1,
    )
    small_t = jnp.pad(state_grads, ((1, -(taps + 2) % 8), (0, model - states)))

    w_sum, layer_out, grad_input, sum_d, sum_t = reduce_all(
        n,
        t_size,
        grads,
        layer_part.reshape(t_size, -1, model),
        grad_normed.reshape(t_size, -1, model),
        residual,
        norm_gain[None],
        cotangent,
        small_d,
        small_t,
    )
    e1 = s1 + slice_width
    e2 = e1 + heads
    v_taps = kernel_value.shape[0]
    last = sum_d[v_taps + 2]
    return (
        layer_out,
        grad_input,
        sum_t[0],
        w_sum[:, :width],
        w_sum[:, width:s1],
        w_sum[:, e1:e2],
        w_sum[:, s1:e1],
        sum_d[:v_taps],
        sum_d[v_taps],
        sum_t[1 : taps + 1, :states],
        sum_t[taps + 1, :states],
        last[:heads],
        last[heads : 2 * heads],
        last[2 * heads : 3 * heads],
        sum_d[v_taps + 1],
        w_sum[:, e2 + fill :],
    )


def solution(mesh):
    in_specs = (
        P(("dp", "tensor"), None),
        P("dp", None),
        P(),
        P("dp", "tensor"),
        P("dp", "tensor"),
        P("dp", "tensor"),
        P("dp", None),
        P(None, "tensor"),
        P("tensor"),
        P(),
        P(),
        P("tensor"),
        P("tensor"),
        P("tensor"),
        P("tensor"),
        P("dp", "tensor"),
        P(("dp", "tensor"), None),
    )
    out_specs = (
        P(("dp", "tensor"), None),
        P(("dp", "tensor"), None),
        P(),
        P("dp", "tensor"),
        P("dp", "tensor"),
        P("dp", "tensor"),
        P("dp", "tensor"),
        P(None, "tensor"),
        P("tensor"),
        P(),
        P(),
        P("tensor"),
        P("tensor"),
        P("tensor"),
        P("tensor"),
        P("dp", "tensor"),
    )
    body = partial(local, mesh.shape["dp"], mesh.shape["tensor"])
    return jax.shard_map(body, mesh=mesh, in_specs=in_specs, out_specs=out_specs, check_vma=False)
```

profile of v0, /device:TPU:4, one launch (start us, length us, event | category | flops | bytes accessed | tf_op | source)
XLA Modules:
  0.0 249.9 jit_solution(1784887653672039579)
XLA Ops:
  1.8 1.9 multiply_convert_fusion.2.a_ref
  3.7 1.8 convert_element_type.55.c_ref
  6.3 1.9 concatenate.39.w_ref
  8.2 59.7 %shard_map.288 = (bf16[4,128,1024]{2,1,0:T(8,128)(2,1)}, bf16[4,128,1024]{2,1,0:T(8,128)(2,1)}, bf16[8,128,1920]{2,1,0:T(8,128)(2,1)}) custom-call(bf16[128,1024]{1,0:T(8,128)(2,1)} %multiply_convert_fusion.2.a_ref, bf16[128,1024]{1,0:T(8,128)(2,1)} %convert_element_type.55.c_ref, bf16[128,1920]{1,0:T(8,128)(2,1)} %concatenate.39.w_ref), custom_call_target="tpu_custom_call" | custom-call | tf_op jit(solution)/shard_map/pallas_call | solution.py:189
  68.1 3.9 %fusion = f32[512,1408]{1,0:T(8,128)S(1)} fusion(bf16[512,1024]{1,0:T(8,128)(2,1)} %bitcast.121, bf16[1024,1920]{1,0:T(8,128)(2,1)} %bitcast.74), kind=kOutput, calls=%fused_computation.2 | convolution fusion | flops 1476395008 | bytes 6815744 | tf_op jit(solution)/shard_map/dot_general | solution.py:750
  72.2 1.8 fusion.10
  78.0 7.8 %shard_map.289 = f32[512,512]{1,0:T(8,128)} custom-call(f32[512,512]{1,0:T(8,128)} %get-tuple-element.111.x_ref, f32[512,128]{1,0:T(8,128)} %get-tuple-element.124.b_ref, f32[512,128]{1,0:T(8,128)} %get-tuple-element.123.c_ref, f32[512,8]{1,0:T(8,128)} %copy.63.cum_ref, f32[8,512]{1,0:T(8,128)} %bitcast.84, f32[512,8]{1,0:T(8,128)} %copy-done.4, ...), custom_call_target="tpu_custom_call" | custom-call | tf_op jit(solution)/shard_map/pallas_call | solution.py:583
  85.8 4.4 %multiply_reduce_fusion.6 = (f32[512]{0:T(512)S(1)}, f32[512]{0:T(512)S(1)}, f32[512,512]{1,0:T(8,128)}, f32[512,512]{1,0:T(8,128)}) fusion(f32[512]{0:T(512)S(1)} %copy-done.24, f32[512,512]{1,0:T(8,128)} %shard_map.289, f32[512,1408]{1,0:T(8,128)} %copy-done, bf16[512,1024]{1,0:T(8,128)(2,1)} %bitcast.123, bf16[1024,1920]{1,0:T(8,128)(2,1)} %bitcast.75), kind=kOutput, calls=%fused_computation.28 | convolution fusion | flops 539491328 | bytes 6297600 | tf_op jit(solution)/shard_map/dot_general | solution.py:775
  90.8 5.0 %shard_map.290 = f32[4,8,128]{2,1,0:T(8,128)} custom-call(f32[8,128]{1,0:T(8,128)} %pad_maximum_fusion.1.x_ref), custom_call_target="tpu_custom_call" | custom-call | tf_op jit(solution)/shard_map/pallas_call | solution.py:223
  96.5 3.5 %convolution_convert_fusion.3 = bf16[1024,512]{1,0:T(8,128)(2,1)} fusion(bf16[512,1024]{1,0:T(8,128)(2,1)} %bitcast.124, f32[512,512]{1,0:T(8,128)} %get-tuple-element.110, f32[512]{0:T(512)S(1)} %get-tuple-element.140, f32[512]{0:T(512)S(1)} %copy-done.24), kind=kOutput, calls=%fused_computation.7 | convolution fusion | flops 538181632 | bytes 3149824 | tf_op jit(solution)/shard_map/dot_general | solution.py:854
  100.0 3.7 %fusion.14 = (f32[512,512]{1,0:T(8,128)}, bf16[512,512]{1,0:T(8,128)(2,1)}, f32[512]{0:T(512)}) fusion(f32[512]{0:T(512)S(1)} %get-tuple-element.139, f32[512,512]{1,0:T(8,128)S(1)} %copy-done.8, f32[512,512]{1,0:T(8,128)S(1)} %copy-done.11, f32[512]{0:T(512)S(1)} %multiply_multiply_fusion.6, f32[512]{0:T(512)S(1)} %get-tuple-element.140, ...), kind=kLoop, calls=%fused_computation.45 | loop fusion | flops 5242368 | bytes 5777408 | tf_op jit(solution)/shard_map/mul | solution.py:792
  103.8 13.9 %shard_map.291 = (f32[512,512]{1,0:T(8,128)}, f32[512,128]{1,0:T(8,128)}, f32[512,128]{1,0:T(8,128)}, f32[512,8]{1,0:T(8,128)}, f32[8,512]{1,0:T(8,128)}, /*index=5*/f32[512,8]{1,0:T(8,128)}, f32[512,8]{1,0:T(8,128)}) custom-call(f32[512,512]{1,0:T(8,128)} %get-tuple-element.111.x_ref, f32[512,512]{1,0:T(8,128)} %get-tuple-element.113.dy_ref, ...), custom_call_target="tpu_custom_call" | custom-call | tf_op jit(solution)/shard_map/pallas_call | solution.py:672
  117.7 3.2 %multiply_reduce_fusion.4 = (f32[512]{0:T(512)S(1)}, f32[512]{0:T(512)S(1)}, f32[512]{0:T(512)S(1)}, f32[512]{0:T(512)}, f32[512]{0:T(512)S(1)}, /*index=5*/f32[512,512]{1,0:T(8,128)S(1)}) fusion(f32[512,512]{1,0:T(8,128)S(1)} %slice.234, f32[512]{0:T(512)S(1)} %get-tuple-element.151, f32[512]{0:T(512)S(1)} %get-tuple-element.150, ...), kind=kLoop, calls=%fused_computation.22 | loop fusion | flops 5502464 | bytes 5259264 | tf_op jit(solution)/shard_map/transpose(jvp())/reduce_sum | solution.py:692
  124.0 8.6 %shard_map.292 = bf16[4,512,64]{2,1,0:T(8,128)(2,1)} custom-call(bf16[4,512,64]{2,1,0:T(8,128)(2,1)} %maximum_bitcast_fusion.x_ref), custom_call_target="tpu_custom_call" | custom-call | tf_op jit(solution)/shard_map/pallas_call | solution.py:223
  135.5 2.6 %fusion.37 = (f32[8]{0:T(128)}, bf16[512,8]{1,0:T(8,128)(2,1)S(1)}, f32[8]{0:T(128)}) fusion(f32[8]{0:T(128)S(1)} %copy-done.31, f32[512,1408]{1,0:T(8,128)} %copy-done, f32[512,8]{1,0:T(8,128)S(1)} %copy-done.34, f32[8]{0:T(128)S(1)} %exponential_negate_fusion, f32[512,8]{1,0:T(8,128)S(1)} %copy-done.5, f32[512,8]{0,1:T(8,128)S(1)} %copy.72, ...), kind=kOutput, calls=%fused_computation.117 | convolution fusion | flops 25743344 | bytes 90240 | tf_op jit(solution)/shard_map/dot_general | solution.py:812
  138.1 1.6 concatenate.45
  139.7 2.9 %convolution_convert_fusion = bf16[1024,1152]{1,0:T(8,128)(2,1)S(1)} fusion(bf16[512,1024]{1,0:T(8,128)(2,1)} %bitcast.122, bf16[512,1152]{1,0:T(8,128)(2,1)S(1)} %concatenate.45), kind=kOutput, calls=%fused_computation | convolution fusion | flops 1209139200 | bytes 4587520 | tf_op jit(solution)/shard_map/dot_general | solution.py:851
  142.6 2.0 pad_maximum_fusion
  146.2 1.7 convolution_convert_fusion.2
  149.9 4.6 %concatenate.47 = bf16[1024,1152]{1,0:T(8,128)(2,1)} concatenate(bf16[1024,1024]{1,0:T(8,128)(2,1)S(1)} %slice.241, bf16[1024,64]{1,0:T(8,128)(2,1)S(1)} %constant_dynamic-slice_fusion, bf16[1024,8]{1,0:T(8,128)(2,1)} %slice.243, bf16[1024,56]{1,0:T(8,128)(2,1)} %broadcast_in_dim.24), dimensions={1} | concatenate | bytes 4718592 | tf_op jit(solution)/shard_map/concatenate | solution.py:842
  154.6 4.3 %convolution_convert_fusion.1 = bf16[512,1024]{1,0:T(8,128)(2,1)} fusion(bf16[512,1152]{1,0:T(8,128)(2,1)S(1)} %concatenate.45, bf16[1024,1152]{1,0:T(8,128)(2,1)} %concatenate.47), kind=kOutput, calls=%fused_computation.5 | convolution fusion | flops 1208483840 | bytes 4587520 | tf_op jit(solution)/shard_map/dot_general | solution.py:845
  160.7 73.4 %shard_map.293 = (f32[128,1664]{1,0:T(8,128)}, f32[128,1024]{1,0:T(8,128)}, f32[128,1024]{1,0:T(8,128)}, f32[8,512]{1,0:T(8,128)}, f32[8,1024]{1,0:T(8,128)}) custom-call(bf16[8,128,1664]{2,1,0:T(8,128)(2,1)} %bitcast.73, bf16[4,128,1024]{2,1,0:T(8,128)(2,1)} %bitcast.80, bf16[4,128,1024]{2,1,0:T(8,128)(2,1)} %bitcast.81, f32[128,1024]{1,0:T(8,128)} %res_ref.1, ...), custom_call_target="tpu_custom_call" | custom-call | tf_op jit(solution)/shard_map/pallas_call | solution.py:493
  235.4 2.0 fusion.39
  247.2 1.9 copy.86
  (138 shorter events, 30.5 us)
Async XLA Ops:
  0.6 67.3 %copy-start.18 = (s32[1,512]{1,0:T(1,128)S(1)}, s32[1,512]{1,0:T(1,128)}, u32[]{:S(2)}) copy-start(s32[1,512]{1,0:T(1,128)} %sr_ref.3) | copy-start | bytes 6148
  0.7 67.4 %copy-start.22 = (f32[4,512]{1,0:T(4,128)S(1)}, f32[4,512]{1,0:T(4,128)}, u32[]{:S(2)}) copy-start(f32[4,512]{1,0:T(4,128)} %param.24) | copy-start | bytes 24580
  68.1 4.1 %copy-start.23 = (f32[512]{0:T(512)S(1)}, f32[512]{0:T(512)}, u32[]{:S(2)}) copy-start(f32[512]{0:T(512)} %param.25) | copy-start | bytes 6148
  75.3 10.4 %copy-start.24 = (f32[512]{0:T(512)S(1)}, f32[512]{0:T(512)}, u32[]{:S(2)}) copy-start(f32[512]{0:T(512)} %param.31) | copy-start | bytes 6148
  90.2 9.9 %copy-start.1 = (f32[512,512]{1,0:T(8,128)S(1)}, f32[512,512]{1,0:T(8,128)}, u32[]{:S(2)}) copy-start(f32[512,512]{1,0:T(8,128)} %shard_map.289) | copy-start | bytes 3145732
  96.5 3.6 %copy-start.8 = (f32[512,512]{1,0:T(8,128)S(1)}, f32[512,512]{1,0:T(8,128)}, u32[]{:S(2)}) copy-start(f32[512,512]{1,0:T(8,128)} %get-tuple-element.110) | copy-start | bytes 3145732
  96.5 3.6 %copy-start.11 = (f32[512,512]{1,0:T(8,128)S(1)}, f32[512,512]{1,0:T(8,128)}, u32[]{:S(2)}) copy-start(f32[512,512]{1,0:T(8,128)} %get-tuple-element.152) | copy-start | bytes 3145732
  123.1 12.3 %copy-start.16 = (f32[512,8]{1,0:T(8,128)S(1)}, f32[512,8]{1,0:T(8,128)}, u32[]{:S(2)}) copy-start(f32[512,8]{1,0:T(8,128)} %get-tuple-element.38) | copy-start | bytes 49156
  124.0 11.5 %copy-start.5 = (f32[512,8]{1,0:T(8,128)S(1)}, f32[512,8]{1,0:T(8,128)}, u32[]{:S(2)}) copy-start(f32[512,8]{1,0:T(8,128)} %copy-done.4) | copy-start | bytes 49156
  124.0 11.5 %copy-start.34 = (f32[512,8]{1,0:T(8,128)S(1)}, f32[512,8]{1,0:T(8,128)}, u32[]{:S(2)}) copy-start(f32[512,8]{1,0:T(8,128)} %get-tuple-element.37) | copy-start | bytes 49156
  124.0 11.5 %copy-start.35 = (f32[8,512]{1,0:T(8,128)S(1)}, f32[8,512]{1,0:T(8,128)}, u32[]{:S(2)}) copy-start(f32[8,512]{1,0:T(8,128)} %get-tuple-element.39) | copy-start | bytes 49156
  142.6 3.3 %copy-start.6 = (bf16[8,128,1920]{2,1,0:T(8,128)(2,1)S(1)}, bf16[8,128,1920]{2,1,0:T(8,128)(2,1)}, u32[]{:S(2)}) copy-start(bf16[8,128,1920]{2,1,0:T(8,128)(2,1)} %get-tuple-element.32) | copy-start | bytes 11796484
  142.6 3.6 %copy-start.9 = (f32[512,512]{1,0:T(8,128)S(1)}, f32[512,512]{1,0:T(8,128)}, u32[]{:S(2)}) copy-start(f32[512,512]{1,0:T(8,128)} %get-tuple-element.110) | copy-start | bytes 3145732
  154.5 4.4 %copy-start.15 = (f32[512,8]{1,0:T(8,128)S(1)}, f32[512,8]{1,0:T(8,128)}, u32[]{:S(2)}) copy-start(f32[512,8]{1,0:T(8,128)} %get-tuple-element.40) | copy-start | bytes 49156
  154.5 4.5 %copy-start.32 = (f32[8]{0:T(128)S(1)}, f32[8]{0:T(128)}, u32[]{:S(2)}) copy-start(f32[8]{0:T(128)} %get-tuple-element.108) | copy-start | bytes 100
  154.5 4.5 %copy-start.33 = (f32[8]{0:T(128)S(1)}, f32[8]{0:T(128)}, u32[]{:S(2)}) copy-start(f32[8]{0:T(128)} %get-tuple-element.125) | copy-start | bytes 100
  154.5 4.6 %copy-start.20 = (f32[512]{0:T(512)S(1)}, f32[512]{0:T(512)}, u32[]{:S(2)}) copy-start(f32[512]{0:T(512)} %get-tuple-element.97) | copy-start | bytes 6148
  154.5 4.6 %copy-start.21 = (f32[512]{0:T(512)S(1)}, f32[512]{0:T(512)}, u32[]{:S(2)}) copy-start(f32[512]{0:T(512)} %get-tuple-element.115) | copy-start | bytes 6148
  154.6 5.2 %copy-start.26 = (f32[64]{0:T(128)S(1)}, f32[64]{0:T(128)}, u32[]{:S(2)}) copy-start(f32[64]{0:T(128)} %get-tuple-element.101) | copy-start | bytes 772
  154.6 5.2 %copy-start.27 = (f32[64]{0:T(128)S(1)}, f32[64]{0:T(128)}, u32[]{:S(2)}) copy-start(f32[64]{0:T(128)} %get-tuple-element.102) | copy-start | bytes 772
  154.6 5.2 %copy-start.28 = (f32[64]{0:T(128)S(1)}, f32[64]{0:T(128)}, u32[]{:S(2)}) copy-start(f32[64]{0:T(128)} %get-tuple-element.103) | copy-start | bytes 772
  154.6 5.2 %copy-start.29 = (f32[64]{0:T(128)S(1)}, f32[64]{0:T(128)}, u32[]{:S(2)}) copy-start(f32[64]{0:T(128)} %get-tuple-element.104) | copy-start | bytes 772
  154.6 5.2 %copy-start.25 = (f32[64]{0:T(128)S(1)}, f32[64]{0:T(128)}, u32[]{:S(2)}) copy-start(f32[64]{0:T(128)} %get-tuple-element.105) | copy-start | bytes 772
  234.0 15.1 %copy-start.12 = (f32[128,1024]{1,0:T(8,128)S(1)}, f32[128,1024]{1,0:T(8,128)}, u32[]{:S(2)}) copy-start(f32[128,1024]{1,0:T(8,128)} %get-tuple-element.173) | copy-start | bytes 1572868
  (13 other events, 29.2 us)
where the time goes:
time: 251 us; the launch traced here: 250 us
  Pallas kernels  168 us (67%)
  local copies, waits for them, and re-layouts  33.5 us (13%)
  matrix products  24 us (10%)
  other arithmetic  22.8 us (9%)
    pallas_call x1, Pallas kernels, reduce_all(): pl.pallas_call(partial(reduce_kernel, n, t_size), out_shape=(struct((rows...  73.4 us
    pallas_call x1, Pallas kernels, gather_all(): pl.pallas_call(partial(gather_kernel, n, t_size), out_shape=(jax.ShapeDty...  59.7 us
    pallas_call x1, Pallas kernels, mix_backward(): pl.pallas_call(partial(back_kernel, width), grid=(pairs,), out_shape=outs...  13.9 us
    pallas_call x2, Pallas kernels, spread_tensor(): pl.pallas_call(partial(spread_kernel, t_size, scatter), out_shape=jax.Sha...  13.6 us
    pallas_call x1, Pallas kernels, mix_forward(): pl.pallas_call(partial(mix_kernel, width), grid=(pairs,), out_shape=jax.S...  7.8 us
    unnamed x79, local copies, waits for them, and re-layouts  7.07 us

commit v1 on v0

--- a/solution.py
+++ b/solution.py
@@ -24,7 +24,7 @@
 
 
 def halves(cols):
-    left = (cols // 128 + 1) // 2 * 128
+    left = cols // 128 * 2 // 5 * 128
     return pl.ds(0, left), pl.ds(left, cols - left)
 
 
@@ -65,13 +65,44 @@
 
 
 def gather_kernel(
-    n, t_size, a_ref, c_ref, w_ref, ga, gc, gw, sa, ra, sc, rc, sx, su, sd, rw
+    n,
+    t_size,
+    res_ref,
+    gain_ref,
+    cot_ref,
+    gate_ref,
+    value_ref,
+    state_ref,
+    step_ref,
+    out_ref,
+    ga,
+    gc,
+    gw,
+    a_ref,
+    c_ref,
+    w_ref,
+    sa,
+    ra,
+    sc,
+    rc,
+    sx,
+    su,
+    sd,
+    rw,
 ):
     d = lax.axis_index("dp")
     t = lax.axis_index("tensor")
     hi = d // 2
     lo = lax.rem(d, 2)
     line = n // 2
+    begin = 0
+    for ref in (gate_ref, value_ref, state_ref):
+        w_ref[:, begin : begin + ref.shape[1]] = ref[...]
+        begin += ref.shape[1]
+    end = w_ref.shape[1] - out_ref.shape[1]
+    w_ref[:, begin:end] = jnp.zeros((w_ref.shape[0], end - begin), BF16)
+    w_ref[:, begin : begin + step_ref.shape[1]] = step_ref[...]
+    w_ref[:, end:] = out_ref[...]
     parts = halves(w_ref.shape[1])
     everything = pl.ds(0, w_ref.shape[0])
     barrier = pltpu.get_barrier_semaphore()
@@ -99,9 +130,6 @@
     has_up = hi < line - 1
     has_down = hi > 0
     own(0, sx, mate).start()
-    for k in range(1, t_size):
-        other = lax.rem(t + k, t_size)
-        push(a_ref, ga.at[t], sa.at[other], ra.at[t], d, other).start()
 
     @pl.when(has_up)
     def _():
@@ -114,6 +142,13 @@
         own(0, sd, d - 2).start()
 
     own(1, sx, mate).start()
+    res = res_ref[...]
+    inv = lax.rsqrt(jnp.mean(res * res, axis=1, keepdims=True) + epsilon)
+    a_ref[...] = (res * inv * gain_ref[...]).astype(BF16)
+    for k in range(1, t_size):
+        other = lax.rem(t + k, t_size)
+        push(a_ref, ga.at[t], sa.at[other], ra.at[t], d, other).start()
+    c_ref[...] = cot_ref[...].astype(BF16)
     for k in range(1, t_size):
         other = lax.rem(t + k, t_size)
         push(c_ref, gc.at[t], sc.at[other], rc.at[t], d, other).start()
@@ -184,20 +219,26 @@
         push(c_ref, gc.at[other], sc.at[other], rc.at[other], d, other).wait()
 
 
-def gather_all(n, t_size, a, c, w):
+def gather_all(n, t_size, res, gain, cot, gate, value, state, step, out):
     dma = pltpu.SemaphoreType.DMA
+    tok = pltpu.VMEM(res.shape, BF16)
+    cols = gate.shape[1] + value.shape[1] + state.shape[1] + out.shape[1]
+    cols += -(-step.shape[1] // 128) * 128
+    shape = (gate.shape[0], cols)
     return pl.pallas_call(
         partial(gather_kernel, n, t_size),
         out_shape=(
-            jax.ShapeDtypeStruct((t_size,) + a.shape, a.dtype),
-            jax.ShapeDtypeStruct((t_size,) + c.shape, c.dtype),
-            jax.ShapeDtypeStruct((n,) + w.shape, w.dtype),
+            jax.ShapeDtypeStruct((t_size,) + res.shape, BF16),
+            jax.ShapeDtypeStruct((t_size,) + res.shape, BF16),
+            jax.ShapeDtypeStruct((n,) + shape, BF16),
         ),
-        in_specs=[VM] * 3,
+        in_specs=[VM] * 8,
         out_specs=(VM, VM, VM),
-        scratch_shapes=[dma((t_size,))] * 4 + [dma((2, n))] * 4,
+        scratch_shapes=[tok, tok, pltpu.VMEM(shape, BF16)]
+        + [dma((t_size,))] * 4
+        + [dma((2, n))] * 4,
         compiler_params=pltpu.CompilerParams(collective_id=0, has_side_effects=True),
-    )(a, c, w)
+    )(res, gain, cot, gate, value, state, step, out)
 
 
 def spread_kernel(t_size, scatter, x_ref, out_ref, ss, rs):
@@ -233,7 +274,8 @@
 def reduce_kernel(
     n,
     t_size,
-    w_ref,
+    wa_ref,
+    wb_ref,
     l_ref,
     g_ref,
     res_ref,
@@ -241,11 +283,23 @@
     cot_ref,
     sd_ref,
     st_ref,
-    w_out,
+    gate_out,
+    value_out,
+    state_out,
+    step_out,
+    proj_out,
     l_out,
     gi_out,
-    sd_out,
-    st_out,
+    norm_out,
+    kv_out,
+    bv_out,
+    gg_out,
+    sb_out,
+    ld_out,
+    sk_out,
+    ks_out,
+    bs_out,
+    acc,
     rl,
     rg,
     rx0,
@@ -293,9 +347,6 @@
     lo = lax.rem(d, 2)
     line = n // 2
     mate = d + 1 - 2 * lo
-    rows = w_ref.shape[1]
-    every = pl.ds(0, rows)
-    top, low = halves(w_ref.shape[2])
     barrier = pltpu.get_barrier_semaphore()
     greet_tensor(t_size, barrier)
     greet_dp(n, barrier)
@@ -305,10 +356,16 @@
 
     def send_x0(k):
         return push(
-            w_ref.at[2 * k + 1 - lo, every, top], rx0.at[k], s_x0.at[k], q_x0.at[k], mate, t
+            wa_ref.at[2 * k + 1 - lo], rx0.at[k], s_x0.at[k], q_x0.at[k], mate, t
         )
 
-    loop(0, line, lambda k: send_x0(k).start())
+    def open_x0(k):
+        send_x0(line - 1 - k).start()
+        send_x0(k).start()
+
+    loop(0, line // 2, open_x0)
+    if line % 2:
+        send_x0(line // 2).start()
 
     def tensor_send(src, buf, ss, qs, other):
         return push(src.at[other], buf.at[t], ss.at[other], qs.at[t], d, other)
@@ -350,12 +407,12 @@
             hop(buf, got, ss, qs, k, to).start()
 
     def pair(k):
-        return w_ref[pl.ds(2 * k, 2), :, low].astype(F32)
+        return wb_ref[pl.ds(2 * k, 2)].astype(F32)
 
     set1 = (pair, bu1, ru1, s_u1, q_u1, bd1, rd1, s_d1, q_d1)
 
     def joined(k):
-        return w_ref[2 * k + lo, :, top].astype(F32) + rx0[k].astype(F32)
+        return wa_ref[2 * k + lo].astype(F32) + rx0[k].astype(F32)
 
     set0 = (joined, bu0, ru0, s_u0, q_u0, bd0, rd0, s_d0, q_d0)
 
@@ -385,31 +442,41 @@
     for k in range(1, t_size):
         st_send(lax.rem(t + k, t_size)).start()
 
-    loop(
-        0,
-        line,
-        lambda k: push(rx0.at[k], rx0.at[k], s_x0.at[k], q_x0.at[k], mate, t).wait_recv(),
-    )
-
+    def got_x0(k):
+        push(rx0.at[k], rx0.at[k], s_x0.at[k], q_x0.at[k], mate, t).wait_recv()
+
+    if line == 1:
+        got_x0(0)
     def walk0(k):
+        @pl.when(2 * k < line - 1)
+        def _():
+            got_x0(line - 1 - k)
+            got_x0(k)
+
+        if line % 2:
+
+            @pl.when(2 * k == line - 1)
+            def _():
+                got_x0(k)
+
         chain(line - 1 - k, set0, True)
         chain(k, set0, False)
 
     loop(0, line - 1, walk0)
 
-    w_out[:, low] = w_ref[d, :, low].astype(F32)
-    bx1[...] = w_ref[mate, :, low]
+    proj_out[...] = wb_ref[d].astype(F32)
+    bx1[...] = wb_ref[mate]
 
     @pl.when(has_down)
     def _():
         hop(bu1, ru1, s_u1, q_u1, hi, d).wait_recv()
-        w_out[:, low] = w_out[:, low] + ru1[hi, lo].astype(F32)
+        proj_out[...] = proj_out[...] + ru1[hi, lo].astype(F32)
         bx1[...] = (bx1[...].astype(F32) + ru1[hi, 1 - lo].astype(F32)).astype(BF16)
 
     @pl.when(has_up)
     def _():
         hop(bd1, rd1, s_d1, q_d1, hi, d).wait_recv()
-        w_out[:, low] = w_out[:, low] + rd1[hi, lo].astype(F32)
+        proj_out[...] = proj_out[...] + rd1[hi, lo].astype(F32)
         bx1[...] = (bx1[...].astype(F32) + rd1[hi, 1 - lo].astype(F32)).astype(BF16)
 
     send_x1 = push(bx1, rx1, s_x1.at[0], q_x1.at[0], mate, t)
@@ -434,20 +501,20 @@
         l_sum = l_sum + rl[other].astype(F32)
     l_out[...] = res_ref[...] + l_sum
 
-    w_out[:, top] = joined(hi)
+    acc[...] = joined(hi)
 
     @pl.when(has_down)
     def _():
         hop(bu0, ru0, s_u0, q_u0, hi, d).wait_recv()
-        w_out[:, top] = w_out[:, top] + ru0[hi].astype(F32)
+        acc[...] = acc[...] + ru0[hi].astype(F32)
 
     @pl.when(has_up)
     def _():
         hop(bd0, rd0, s_d0, q_d0, hi, d).wait_recv()
-        w_out[:, top] = w_out[:, top] + rd0[hi].astype(F32)
+        acc[...] = acc[...] + rd0[hi].astype(F32)
 
     send_x1.wait()
-    w_out[:, low] = w_out[:, low] + rx1[...].astype(F32)
+    proj_out[...] = proj_out[...] + rx1[...].astype(F32)
 
     rsd[d] = sd_ref[...]
     rst_dp[d] = st_sum[...]
@@ -458,8 +525,24 @@
         push(st_sum, rst_dp.at[q], s_sp.at[q], q_sp.at[q], q, t).wait()
 
     loop(1, n, settle)
-    sd_out[...] = jnp.sum(rsd[...], axis=0)
-    st_out[...] = jnp.sum(rst_dp[...], axis=0)
+    sums_d = jnp.sum(rsd[...], axis=0)
+    sums_t = jnp.sum(rst_dp[...], axis=0)
+    taps = kv_out.shape[0]
+    kv_out[...] = sums_d[:taps]
+    bv_out[...] = sums_d[taps : taps + 1]
+    gg_out[...] = sums_d[taps + 1 : taps + 2]
+    heads = step_out.shape[1]
+    for i, ref in enumerate((sb_out, ld_out, sk_out)):
+        ref[...] = sums_d[taps + 2 + i : taps + 3 + i, :heads]
+    taps = ks_out.shape[0]
+    states = ks_out.shape[1]
+    norm_out[...] = sums_t[:1]
+    ks_out[...] = sums_t[1 : taps + 1, :states]
+    bs_out[...] = sums_t[taps + 1 : taps + 2, :states]
+    begin = 0
+    for ref in (gate_out, value_out, state_out, step_out):
+        ref[...] = acc[:, begin : begin + ref.shape[1]]
+        begin += ref.shape[1]
 
     def drain(k):
         send_x0(k).wait_send()
@@ -477,13 +560,15 @@
     loop(0, line, drain)
 
 
-def reduce_all(n, t_size, w, l, g, res, gain, cot, small_d, small_t):
+def reduce_all(n, t_size, wa, wb, l, g, res, gain, cot, small_d, small_t, dims):
+    width, slice_width, heads, v_taps, s_taps, states = dims
     dma = pltpu.SemaphoreType.DMA
     vm = pltpu.VMEM
-    rows, cols = w.shape[1:]
+    rows, left = wa.shape[1:]
+    right = wb.shape[2]
+    model = res.shape[1]
     line = n // 2
-    left = halves(cols)[0].size
-    two = vm((line, 2, rows, cols - left), BF16)
+    two = vm((line, 2, rows, right), BF16)
     one = vm((line, rows, left), BF16)
     tok = vm(l.shape, BF16)
     struct = jax.ShapeDtypeStruct
@@ -493,19 +578,31 @@
     return pl.pallas_call(
         partial(reduce_kernel, n, t_size),
         out_shape=(
-            struct((rows, cols), F32),
+            struct((rows, width), F32),
+            struct((rows, width), F32),
+            struct((rows, slice_width), F32),
+            struct((rows, heads), F32),
+            struct((rows, right), F32),
             struct(res.shape, F32),
             struct(res.shape, F32),
-            struct(small_d.shape, F32),
-            struct(small_t.shape, F32),
+            struct((1, model), F32),
+            struct((v_taps, width), F32),
+            struct((1, width), F32),
+            struct((1, width), F32),
+            struct((1, heads), F32),
+            struct((1, heads), F32),
+            struct((1, heads), F32),
+            struct((s_taps, states), F32),
+            struct((1, states), F32),
         ),
-        in_specs=[VM] * 8,
-        out_specs=(VM,) * 5,
+        in_specs=[VM] * 9,
+        out_specs=(VM,) * 16,
         scratch_shapes=[
+            vm((rows, left), F32),
             tok,
             tok,
             one,
-            vm((rows, cols - left), BF16),
+            vm((rows, right), BF16),
             two,
             two,
             one,
@@ -514,7 +611,7 @@
             two,
             one,
             one,
-            vm((rows, cols - left), BF16),
+            vm((rows, right), BF16),
             vm(small_t.shape, F32),
             vm((t_size,) + small_t.shape, F32),
             vm(small_t.shape, F32),
@@ -528,7 +625,7 @@
         + [t_sem] * 2
         + [n_sem] * 4,
         compiler_params=pltpu.CompilerParams(collective_id=3, has_side_effects=True),
-    )(w, l, g, res, gain, cot, small_d, small_t)
+    )(wa, wb, l, g, res, gain, cot, small_d, small_t)
 
 
 def dot_f(a, b, dims, precision=None):
@@ -724,25 +821,22 @@
     tokens = seg_ids.shape[0]
     t = lax.axis_index("tensor")
 
-    inv = lax.rsqrt(jnp.mean(residual * residual, axis=1, keepdims=True) + epsilon)
-    normed = (residual * inv * norm_gain).astype(BF16)
-    cot_half = cotangent.astype(BF16)
     step_pad = -heads % 128
-    w_mine = jnp.concatenate(
-        [
-            in_gate,
-            in_value,
-            in_state,
-            in_step,
-            jnp.zeros((rows, step_pad), BF16),
-            out_proj,
-        ],
-        axis=1,
-    )
-    full_rows, cot_full, w_full = gather_all(n, t_size, normed, cot_half, w_mine)
+    full_rows, cot_full, w_full = gather_all(
+        n,
+        t_size,
+        residual,
+        norm_gain[None],
+        cotangent,
+        in_gate,
+        in_value,
+        in_state,
+        in_step,
+        out_proj,
+    )
     full_rows = full_rows.reshape(tokens, model)
     cot_full = cot_full.reshape(tokens, model)
-    w_full = w_full.reshape(model, w_mine.shape[1])
+    w_full = w_full.reshape(model, w_full.shape[2])
     s1, s2 = 2 * width, 2 * width + states
     s3 = s2 + heads
     out_full = w_full[:, s3 + step_pad :]
@@ -805,9 +899,11 @@
     )
     slice_width = states // t_size
     grad_bc = jnp.concatenate([grad_b, grad_c], axis=1).astype(BF16)
-    pieces = grad_bc.reshape(tokens, t_size, slice_width).transpose(1, 0, 2)
-    grad_conv_state = jnp.sum(
-        spread_tensor(t_size, pieces, True, 2).astype(F32), axis=0
+    pieces = grad_bc.reshape(2, tokens // 2, t_size, slice_width).transpose(2, 1, 0, 3)
+    pieces = pieces.reshape(t_size, tokens // 2, 2 * slice_width)
+    packed = jnp.sum(spread_tensor(t_size, pieces, True, 2).astype(F32), axis=0)
+    grad_conv_state = jnp.concatenate(
+        [packed[:, :slice_width], packed[:, slice_width:]], axis=0
     )
     d_keep = lax.dot_general(
         tri, row_e - col_e.T, (((0,), (0,)), ((), ())), precision=precise
@@ -854,12 +950,10 @@
     grad_out = lax.dot_general(
         cot_full, gate_normed, (((0,), (0,)), ((), ())), preferred_element_type=F32
     ).astype(BF16)
-    grads = jnp.concatenate([grad_weights, grad_out], axis=1).reshape(n, rows, -1)
-
-    misc = jnp.concatenate([grad_step_bias, grad_log_decay, grad_skip])
-    misc = jnp.pad(misc, (0, width - misc.shape[0]))
+    misc = jnp.stack([grad_step_bias, grad_log_decay, grad_skip])
+    misc = jnp.pad(misc, ((0, 0), (0, width - heads)))
     small_d = jnp.concatenate(
-        [grad_kernel_value, grad_bias_value[None], grad_gate_gain[None], misc[None]], axis=0
+        [grad_kernel_value, grad_bias_value[None], grad_gate_gain[None], misc], axis=0
     )
     small_d = jnp.pad(small_d, ((0, -small_d.shape[0] % 8), (0, 0)))
     taps = kernel_state.shape[0]
@@ -871,10 +965,28 @@
     )
     small_t = jnp.pad(state_grads, ((1, -(taps + 2) % 8), (0, model - states)))
 
-    w_sum, layer_out, grad_input, sum_d, sum_t = reduce_all(
+    (
+        sum_gate,
+        sum_value,
+        sum_state,
+        sum_step,
+        sum_out,
+        layer_out,
+        grad_input,
+        sum_norm,
+        sum_kv,
+        sum_bv,
+        sum_gg,
+        sum_sb,
+        sum_ld,
+        sum_sk,
+        sum_ks,
+        sum_bs,
+    ) = reduce_all(
         n,
         t_size,
-        grads,
+        grad_weights.reshape(n, rows, -1),
+        grad_out.reshape(n, rows, -1),
         layer_part.reshape(t_size, -1, model),
         grad_normed.reshape(t_size, -1, model),
         residual,
@@ -882,28 +994,25 @@
         cotangent,
         small_d,
         small_t,
-    )
-    e1 = s1 + slice_width
-    e2 = e1 + heads
-    v_taps = kernel_value.shape[0]
-    last = sum_d[v_taps + 2]
+        (width, slice_width, heads, kernel_value.shape[0], taps, states),
+    )
     return (
         layer_out,
         grad_input,
-        sum_t[0],
-        w_sum[:, :width],
-        w_sum[:, width:s1],
-        w_sum[:, e1:e2],
-        w_sum[:, s1:e1],
-        sum_d[:v_taps],
-        sum_d[v_taps],
-        sum_t[1 : taps + 1, :states],
-        sum_t[taps + 1, :states],
-        last[:heads],
-        last[heads : 2 * heads],
-        last[2 * heads : 3 * heads],
-        sum_d[v_taps + 1],
-        w_sum[:, e2 + fill :],
+        sum_norm[0],
+        sum_gate,
+        sum_value,
+        sum_step,
+        sum_state,
+        sum_kv,
+        sum_bv[0],
+        sum_ks,
+        sum_bs[0],
+        sum_sb[0],
+        sum_ld[0],
+        sum_sk[0],
+        sum_gg[0],
+        sum_out,
     )
 
 

time: 251 us -> 230 us (0.916)
  Pallas kernels: 168 us -> 155 us
  other arithmetic: 22.8 us -> 16.4 us
  local copies, waits for them, and re-layouts: 33.5 us -> 30.9 us
    slice x9 -> x1, local copies, waits for them, and re-layouts: 11.8 us -> 0.09 us  [local(): packed[:, :slice_width]]
    unnamed x79 -> x105, local copies, waits for them, and re-layouts: 7.07 us -> 16.8 us
    pallas_call x1, Pallas kernels: 73.4 us -> 65.6 us  [reduce_all(): pl.pallas_call(partial(reduce_kernel, n, t_size), out_shape=(struct((rows...]
    pallas_call x1, Pallas kernels: 59.7 us -> 55.8 us  [gather_all(): pl.pallas_call(partial(gather_kernel, n, t_size), out_shape=(jax.ShapeDty...]
    convert_element_type x2 -> x0, other arithmetic: 3.65 us -> none  [the longest x1 1.87 us: local(): normed = (residual * inv * norm_gain).astype(BF16)]
where the time goes in v1:
time: 230 us; the launch traced here: 227 us
  Pallas kernels  155 us (67%)
  local copies, waits for them, and re-layouts  30.9 us (13%)
  matrix products  23.9 us (10%)
  other arithmetic  16.4 us (7%)
    pallas_call x1, Pallas kernels, reduce_all(): pl.pallas_call(partial(reduce_kernel, n, t_size), out_shape=(struct((rows...  65.6 us
    pallas_call x1, Pallas kernels, gather_all(): pl.pallas_call(partial(gather_kernel, n, t_size), out_shape=(jax.ShapeDty...  55.8 us
    unnamed x105, local copies, waits for them, and re-layouts  16.8 us
    pallas_call x1, Pallas kernels, mix_backward(): pl.pallas_call(partial(back_kernel, width), grid=(pairs,), out_shape=outs...  13.8 us
    pallas_call x2, Pallas kernels, spread_tensor(): pl.pallas_call(partial(spread_kernel, t_size, scatter), out_shape=jax.Sha...  11.7 us
    pallas_call x1, Pallas kernels, mix_forward(): pl.pallas_call(partial(mix_kernel, width), grid=(pairs,), out_shape=jax.S...  7.78 us

profile of v1, /device:TPU:4, one launch (start us, length us, event | category | flops | bytes accessed | tf_op | source)
XLA Modules:
  0.0 227.3 jit_solution(9535353155648612763)
XLA Ops:
  0.6 1.4 copy.59.step_ref
  2.0 55.8 %shard_map.288 = (bf16[4,128,1024]{2,1,0:T(8,128)(2,1)}, bf16[4,128,1024]{2,1,0:T(8,128)(2,1)}, bf16[8,128,1920]{2,1,0:T(8,128)(2,1)}) custom-call(f32[128,1024]{1,0:T(8,128)} %res_ref.3, f32[1,1024]{1,0:T(1,128)} %bitcast.97, f32[128,1024]{1,0:T(8,128)} %cot_ref.3, bf16[128,512]{1,0:T(8,128)(2,1)} %gate_ref.1, bf16[128,512]{1,0:T(8,128)(2,1)} %value_ref.1, ...), custom_call_target="tpu_custom_call" | custom-call | tf_op jit(solution)/shard_map/pallas_call | solution.py:228
  59.6 3.9 %fusion = f32[512,1408]{1,0:T(8,128)S(1)} fusion(bf16[512,1024]{1,0:T(8,128)(2,1)} %bitcast.127, bf16[1024,1920]{1,0:T(8,128)(2,1)} %bitcast.74), kind=kOutput, calls=%fused_computation.1 | convolution fusion | flops 1476395008 | bytes 6815744 | tf_op jit(solution)/shard_map/dot_general | solution.py:844
  63.7 1.8 fusion.10
  69.6 7.8 %shard_map.289 = f32[512,512]{1,0:T(8,128)} custom-call(f32[512,512]{1,0:T(8,128)} %get-tuple-element.133.x_ref, f32[512,128]{1,0:T(8,128)} %get-tuple-element.143.b_ref, f32[512,128]{1,0:T(8,128)} %get-tuple-element.142.c_ref, f32[512,8]{1,0:T(8,128)} %copy.61.cum_ref, f32[8,512]{1,0:T(8,128)} %bitcast.85, f32[512,8]{1,0:T(8,128)} %copy-done.4, ...), custom_call_target="tpu_custom_call" | custom-call | tf_op jit(solution)/shard_map/pallas_call | solution.py:680
  77.4 4.5 %multiply_reduce_fusion.6 = (f32[512]{0:T(512)S(1)}, f32[512]{0:T(512)S(1)}, f32[512,512]{1,0:T(8,128)}, f32[512,512]{1,0:T(8,128)}) fusion(f32[512]{0:T(512)S(1)} %copy-done.24, f32[512,512]{1,0:T(8,128)} %shard_map.289, f32[512,1408]{1,0:T(8,128)} %copy-done, bf16[512,1024]{1,0:T(8,128)(2,1)} %bitcast.125, bf16[1024,1920]{1,0:T(8,128)(2,1)} %bitcast.75), kind=kOutput, calls=%fused_computation.26 | convolution fusion | flops 539491328 | bytes 6297600 | tf_op jit(solution)/shard_map/dot_general | solution.py:869
  82.5 5.0 %shard_map.290 = f32[4,8,128]{2,1,0:T(8,128)} custom-call(f32[8,128]{1,0:T(8,128)} %pad_maximum_fusion.2.x_ref), custom_call_target="tpu_custom_call" | custom-call | tf_op jit(solution)/shard_map/pallas_call | solution.py:264
  88.2 4.3 %fusion.14 = (f32[512,512]{1,0:T(8,128)}, bf16[512,512]{1,0:T(8,128)(2,1)}, f32[512]{0:T(512)}) fusion(f32[512]{0:T(512)S(1)} %get-tuple-element.156, f32[512,512]{1,0:T(8,128)} %get-tuple-element.132, f32[512,512]{1,0:T(8,128)} %get-tuple-element.168, f32[512]{0:T(512)S(1)} %multiply_multiply_fusion.6, f32[512]{0:T(512)S(1)} %get-tuple-element.155, ...), kind=kLoop, calls=%fused_computation.43 | loop fusion | flops 5242368 | bytes 5777408 | tf_op jit(solution)/shard_map/mul | solution.py:886
  92.5 13.8 %shard_map.291 = (f32[512,512]{1,0:T(8,128)}, f32[512,128]{1,0:T(8,128)}, f32[512,128]{1,0:T(8,128)}, f32[512,8]{1,0:T(8,128)}, f32[8,512]{1,0:T(8,128)}, /*index=5*/f32[512,8]{1,0:T(8,128)}, f32[512,8]{1,0:T(8,128)}) custom-call(f32[512,512]{1,0:T(8,128)} %get-tuple-element.133.x_ref, f32[512,512]{1,0:T(8,128)} %get-tuple-element.135.dy_ref, ...), custom_call_target="tpu_custom_call" | custom-call | tf_op jit(solution)/shard_map/pallas_call | solution.py:769
  106.4 3.2 %multiply_reduce_fusion.4 = (f32[512]{0:T(512)S(1)}, f32[512]{0:T(512)S(1)}, f32[512]{0:T(512)S(1)}, f32[512]{0:T(512)}, f32[512]{0:T(512)S(1)}, /*index=5*/f32[512,512]{1,0:T(8,128)S(1)}) fusion(f32[512,512]{1,0:T(8,128)S(1)} %slice.170, f32[512]{0:T(512)S(1)} %get-tuple-element.167, f32[512]{0:T(512)S(1)} %get-tuple-element.166, ...), kind=kLoop, calls=%fused_computation.21 | loop fusion | flops 5502464 | bytes 5259264 | tf_op jit(solution)/shard_map/transpose(jvp())/reduce_sum | solution.py:789
  112.5 6.7 %shard_map.292 = bf16[4,256,128]{2,1,0:T(8,128)(2,1)} custom-call(bf16[4,256,128]{2,1,0:T(8,128)(2,1)} %copy.68.x_ref), custom_call_target="tpu_custom_call" | custom-call | tf_op jit(solution)/shard_map/pallas_call | solution.py:264
  122.0 2.6 %fusion.37 = (f32[8]{0:T(128)}, bf16[512,8]{1,0:T(8,128)(2,1)S(1)}, f32[8]{0:T(128)}) fusion(f32[8]{0:T(128)S(1)} %copy-done.34, f32[512,1408]{1,0:T(8,128)} %copy-done, f32[512,8]{1,0:T(8,128)S(1)} %copy-done.38, f32[8]{0:T(128)S(1)} %exponential_negate_fusion, f32[512,8]{1,0:T(8,128)S(1)} %copy-done.5, f32[512,8]{0,1:T(8,128)S(1)} %copy.69, ...), kind=kOutput, calls=%fused_computation.111 | convolution fusion | flops 25743344 | bytes 90240 | tf_op jit(solution)/shard_map/dot_general | solution.py:908
  124.6 1.6 concatenate.32
  126.2 4.3 %convolution_convert_fusion = bf16[1024,1152]{1,0:T(8,128)(2,1)} fusion(bf16[512,1024]{1,0:T(8,128)(2,1)} %bitcast.128, bf16[512,1152]{1,0:T(8,128)(2,1)S(1)} %concatenate.32), kind=kOutput, calls=%fused_computation | convolution fusion | flops 1209139200 | bytes 4587520 | tf_op jit(solution)/shard_map/dot_general | solution.py:947
  130.6 1.8 convolution_convert_fusion.3
  132.4 1.8 convolution_convert_fusion.2
  136.1 4.6 %concatenate.33 = bf16[1024,1152]{1,0:T(8,128)(2,1)} concatenate(bf16[1024,1024]{1,0:T(8,128)(2,1)S(1)} %slice.179, bf16[1024,64]{1,0:T(8,128)(2,1)S(1)} %constant_dynamic-slice_fusion, bf16[1024,8]{1,0:T(8,128)(2,1)} %slice.181, bf16[1024,56]{1,0:T(8,128)(2,1)} %broadcast_in_dim.20), dimensions={1} | concatenate | bytes 4718592 | tf_op jit(solution)/shard_map/concatenate | solution.py:938
  140.8 4.3 %convolution_convert_fusion.1 = bf16[512,1024]{1,0:T(8,128)(2,1)} fusion(bf16[512,1152]{1,0:T(8,128)(2,1)S(1)} %concatenate.32, bf16[1024,1152]{1,0:T(8,128)(2,1)} %concatenate.33), kind=kOutput, calls=%fused_computation.4 | convolution fusion | flops 1208483840 | bytes 4587520 | tf_op jit(solution)/shard_map/dot_general | solution.py:941
  146.8 65.6 %shard_map.293 = (f32[128,512]{1,0:T(8,128)}, f32[128,512]{1,0:T(8,128)}, f32[128,64]{1,0:T(8,128)}, f32[128,8]{1,0:T(8,128)}, f32[128,512]{1,0:T(8,128)}, /*ind...) custom-call(bf16[8,128,1152]{2,1,0:T(8,128)(2,1)} %bitcast.73, ...), custom_call_target="tpu_custom_call" | custom-call | tf_op jit(solution)/shard_map/pallas_call | solution.py:578
  212.6 1.6 copy.74
  214.2 1.5 copy.75
  215.7 1.9 copy.93
  217.6 1.9 copy.94
  219.5 1.3 copy.95
  (149 shorter events, 22.9 us)
Async XLA Ops:
  67.2 10.2 %copy-start.24 = (f32[512]{0:T(512)S(1)}, f32[512]{0:T(512)}, u32[]{:S(2)}) copy-start(f32[512]{0:T(512)} %param.31) | copy-start | bytes 6148
  77.4 10.8 %copy-start.1 = (f32[512,512]{1,0:T(8,128)S(1)}, f32[512,512]{1,0:T(8,128)}, u32[]{:S(2)}) copy-start(f32[512,512]{1,0:T(8,128)} %shard_map.289) | copy-start | bytes 3145732
  112.5 9.4 %copy-start.12 = (f32[512,8]{1,0:T(8,128)S(1)}, f32[512,8]{1,0:T(8,128)}, u32[]{:S(2)}) copy-start(f32[512,8]{1,0:T(8,128)} %get-tuple-element.49) | copy-start | bytes 49156
  126.2 6.2 %copy-start.6 = (bf16[8,128,1920]{2,1,0:T(8,128)(2,1)S(1)}, bf16[8,128,1920]{2,1,0:T(8,128)(2,1)}, u32[]{:S(2)}) copy-start(bf16[8,128,1920]{2,1,0:T(8,128)(2,1)} %get-tuple-element.43) | copy-start | bytes 11796484
  140.7 4.5 %copy-start.35 = (f32[8]{0:T(128)S(1)}, f32[8]{0:T(128)}, u32[]{:S(2)}) copy-start(f32[8]{0:T(128)} %get-tuple-element.130) | copy-start | bytes 100
  140.7 4.5 %copy-start.36 = (f32[8]{0:T(128)S(1)}, f32[8]{0:T(128)}, u32[]{:S(2)}) copy-start(f32[8]{0:T(128)} %get-tuple-element.144) | copy-start | bytes 100
  140.7 4.6 %copy-start.19 = (f32[512]{0:T(512)S(1)}, f32[512]{0:T(512)}, u32[]{:S(2)}) copy-start(f32[512]{0:T(512)} %get-tuple-element.119) | copy-start | bytes 6148
  140.7 4.6 %copy-start.20 = (f32[512]{0:T(512)S(1)}, f32[512]{0:T(512)}, u32[]{:S(2)}) copy-start(f32[512]{0:T(512)} %get-tuple-element.137) | copy-start | bytes 6148
  140.7 5.2 %copy-start.26 = (f32[64]{0:T(128)S(1)}, f32[64]{0:T(128)}, u32[]{:S(2)}) copy-start(f32[64]{0:T(128)} %get-tuple-element.123) | copy-start | bytes 772
  140.7 5.2 %copy-start.27 = (f32[64]{0:T(128)S(1)}, f32[64]{0:T(128)}, u32[]{:S(2)}) copy-start(f32[64]{0:T(128)} %get-tuple-element.124) | copy-start | bytes 772
  140.7 5.2 %copy-start.28 = (f32[64]{0:T(128)S(1)}, f32[64]{0:T(128)}, u32[]{:S(2)}) copy-start(f32[64]{0:T(128)} %get-tuple-element.125) | copy-start | bytes 772
  140.8 5.2 %copy-start.29 = (f32[64]{0:T(128)S(1)}, f32[64]{0:T(128)}, u32[]{:S(2)}) copy-start(f32[64]{0:T(128)} %get-tuple-element.126) | copy-start | bytes 772
  140.8 5.2 %copy-start.25 = (f32[64]{0:T(128)S(1)}, f32[64]{0:T(128)}, u32[]{:S(2)}) copy-start(f32[64]{0:T(128)} %get-tuple-element.127) | copy-start | bytes 772
  212.4 8.3 %copy-start.15 = (f32[128,512]{1,0:T(8,128)S(1)}, f32[128,512]{1,0:T(8,128)}, u32[]{:S(2)}) copy-start(f32[128,512]{1,0:T(8,128)} %get-tuple-element.191) | copy-start | bytes 786436
  212.5 9.0 %copy-start.14 = (f32[128,512]{1,0:T(8,128)S(1)}, f32[128,512]{1,0:T(8,128)}, u32[]{:S(2)}) copy-start(f32[128,512]{1,0:T(8,128)} %get-tuple-element.192) | copy-start | bytes 786436
  212.5 9.7 %copy-start.21 = (f32[4,512]{1,0:T(4,128)S(1)}, f32[4,512]{1,0:T(4,128)}, u32[]{:S(2)}) copy-start(f32[4,512]{1,0:T(4,128)} %get-tuple-element.195) | copy-start | bytes 24580
  212.5 10.3 %copy-start.31 = (f32[1,512]{1,0:T(1,128)S(1)}, f32[1,512]{1,0:T(1,128)}, u32[]{:S(2)}) copy-start(f32[1,512]{1,0:T(1,128)} %get-tuple-element.60) | copy-start | bytes 6148
  212.5 10.8 %copy-start.22 = (f32[4,256]{1,0:T(4,128)S(1)}, f32[4,256]{1,0:T(4,128)}, u32[]{:S(2)}) copy-start(f32[4,256]{1,0:T(4,128)} %get-tuple-element.197) | copy-start | bytes 12292
  212.5 11.4 %copy-start.33 = (f32[1,256]{1,0:T(1,128)S(1)}, f32[1,256]{1,0:T(1,128)}, u32[]{:S(2)}) copy-start(f32[1,256]{1,0:T(1,128)} %get-tuple-element.62) | copy-start | bytes 3076
  212.5 12.0 %copy-start.43 = (f32[1,8]{1,0:T(1,128)S(1)}, f32[1,8]{1,0:T(1,128)}, u32[]{:S(2)}) copy-start(f32[1,8]{1,0:T(1,128)} %get-tuple-element.63) | copy-start | bytes 100
  212.5 12.5 %copy-start.42 = (f32[1,8]{1,0:T(1,128)S(1)}, f32[1,8]{1,0:T(1,128)}, u32[]{:S(2)}) copy-start(f32[1,8]{1,0:T(1,128)} %get-tuple-element.64) | copy-start | bytes 100
  212.5 13.0 %copy-start.41 = (f32[1,8]{1,0:T(1,128)S(1)}, f32[1,8]{1,0:T(1,128)}, u32[]{:S(2)}) copy-start(f32[1,8]{1,0:T(1,128)} %get-tuple-element.65) | copy-start | bytes 100
  212.5 13.5 %copy-start.30 = (f32[1,512]{1,0:T(1,128)S(1)}, f32[1,512]{1,0:T(1,128)}, u32[]{:S(2)}) copy-start(f32[1,512]{1,0:T(1,128)} %get-tuple-element.66) | copy-start | bytes 6148
  212.5 14.1 %copy-start.13 = (f32[128,512]{1,0:T(8,128)S(1)}, f32[128,512]{1,0:T(8,128)}, u32[]{:S(2)}) copy-start(f32[128,512]{1,0:T(8,128)} %get-tuple-element.203) | copy-start | bytes 786436
  (20 other events, 51.1 us)
